TPU v7x, 32 devices: a whole 2x2x4 slice. The times are simulated.
32 devices in a mesh: view: 16 (over z, y, x), head: 2 (over core).
Axes of the slice: x: 2, y: 2, z: 4, core: 2. Of those that a mesh axis runs over, the one named last changes fastest.
Arguments:
- query_tokens: bfloat16 [4096, 1024], P('view'), may hold values from -360 to 360
- image_tokens: bfloat16 [16384, 1024], P('view'), may hold values from -6 to 6
- w_query: bfloat16 [1024, 1024], P(None, 'head'), may hold values from -0.1875 to 0.1875
- w_key: bfloat16 [1024, 1024], P(None, 'head'), may hold values from -0.1875 to 0.1875
- w_value: bfloat16 [1024, 1024], P(None, 'head'), may hold values from -0.1875 to 0.1875
- w_out: bfloat16 [1024, 1024], P('head'), may hold values from -0.1875 to 0.1875
- vis_list: int32 [32, 12], P('view'), may hold values from 0 to 127, as said below
- vis_count: int32 [32], P('view'), may hold values from 8 to 12
Outputs:
- attended: bfloat16 [4096, 1024], P('view', 'head')
Inputs may be any that keep to these rules, and one draw needn't show every extreme that they name: `vis_list`: entry j of row b names a global image block (block g holds image tokens g * 128 onward); the first vis_count[b] entries are the visible ones, the rest padding. All entries of one row lie on different devices of view. Among all entries of the 2 rows held by one device, those lying on one source device name the same block.
All inputs are finite; a program needn't handle non-finite values.
Results may differ from a plain program's by a relative error of at most 0.0085.
The roundings to bfloat16 on the way count: a program that leaves them out, or rounds other values in their place, can miss the bound.
Values may be sent and summed in bfloat16 or wider, within the bound.
A program may use at most 64 MiB of HBM per device.

v0:
```python
import math
import jax
import jax.numpy as jnp
from jax import lax
from jax.sharding import PartitionSpec as P

HEAD_DIM = 128
BLOCK = 128


def attend(query_heads, key_rows, visible, panel_width, head_count):
    groups, length = (key_rows.shape[0], key_rows.shape[1])
    key_heads = key_rows[:, :, :panel_width].reshape(groups, length, head_count, HEAD_DIM)
    value_heads = key_rows[:, :, panel_width:].reshape(groups, length, head_count, HEAD_DIM)
    scores = jnp.einsum(
        "qihd,qkhd->qhik", query_heads, key_heads, preferred_element_type=jnp.float32
    )
    scores = scores * (1.0 / math.sqrt(HEAD_DIM))
    allowed = visible[:, None, None, :]
    peak = jnp.max(jnp.where(allowed, scores, -1e30), axis=3, keepdims=True)
    raised = jnp.where(allowed, jnp.exp(scores - peak), 0.0)
    probs = (raised / jnp.sum(raised, axis=3, keepdims=True)).astype(jnp.bfloat16)
    context = jnp.einsum("qhik,qkhd->qihd", probs, value_heads, preferred_element_type=jnp.float32)
    return context.astype(jnp.bfloat16)


def per_device(query_tokens, image_tokens, w_query, w_key, w_value, w_out, vis_list, vis_count):
    view_count = lax.axis_size("view")
    panel_width = w_query.shape[1]
    head_count = panel_width // HEAD_DIM
    block_count = image_tokens.shape[0] // BLOCK
    query_blocks = vis_list.shape[0]
    queries = jnp.dot(query_tokens, w_query, preferred_element_type=jnp.float32).astype(
        jnp.bfloat16
    )
    image_keys = jnp.dot(image_tokens, w_key, preferred_element_type=jnp.float32).astype(
        jnp.bfloat16
    )
    image_values = jnp.dot(image_tokens, w_value, preferred_element_type=jnp.float32).astype(
        jnp.bfloat16
    )
    image_tiles = jnp.concatenate([image_keys, image_values], axis=1).reshape(
        block_count, BLOCK, 2 * panel_width
    )
    source = vis_list // block_count
    local_index = vis_list % block_count
    listed = jnp.arange(vis_list.shape[1], dtype=jnp.int32)[None, :] < vis_count[:, None]
    view_ids = jnp.arange(view_count, dtype=jnp.int32)
    matches = source[:, :, None] == view_ids[None, None, :]
    wanted = jnp.sum(jnp.where(matches, local_index[:, :, None], 0), axis=1)
    sourced = jnp.any(matches & listed[:, :, None], axis=1)
    asked_ids = lax.all_to_all(wanted, "view", split_axis=1, concat_axis=1, tiled=True)
    picked = jnp.take(image_tiles, asked_ids, axis=0)
    arrived = lax.all_to_all(picked, "view", split_axis=1, concat_axis=1, tiled=True)
    groups = arrived.shape[0]
    query_heads = queries.reshape(query_blocks, BLOCK, head_count, HEAD_DIM)
    key_rows = arrived.reshape(groups, -1, 2 * panel_width)
    visible = jnp.repeat(sourced, BLOCK, axis=1)
    context = attend(query_heads, key_rows, visible, panel_width, head_count)
    context = context.reshape(query_blocks * BLOCK, panel_width)
    partial_value = jnp.dot(context, w_out, preferred_element_type=jnp.float32)
    return lax.psum_scatter(partial_value, "head", scatter_dimension=1, tiled=True).astype(
        jnp.bfloat16
    )


def solution(mesh):
    return jax.shard_map(
        per_device,
        mesh=mesh,
        in_specs=(
            P("view", None),
            P("view", None),
            P(None, "head"),
            P(None, "head"),
            P(None, "head"),
            P("head", None),
            P("view", None),
            P("view"),
        ),
        out_specs=P("view", "head"),
        check_vma=False,
    )
```

profile of v0, /device:TPU:0, one launch (start us, length us, event | category | flops | bytes accessed | tf_op | source)
XLA Modules:
  0.0 303.1 jit_solution(4576486626460102009)
XLA Ops:
  6.5 0.0 copy-start
  6.5 0.0 copy-start.5
  6.5 0.8 and_select_fusion.1
  7.4 0.1 select_reduce_fusion.1
  7.5 0.7 copy.27
  8.2 8.3 %all-to-all-start = ((s32[2,16,1]{0,2,1:T(1,128)}), s32[2,16,1]{0,2,1:T(1,128)S(1)}, u32[]{:S(2)}, u32[]{:S(2)}) async-start(s32[2,16,1]{0,2,1:T(1,128)} %copy.27), calls=%async_computation | async-start | bytes 16384 | tf_op jit(solution)/shard_map/all_to_all | solution.py:52
  16.5 0.0 copy-done
  16.5 2.5 convolution_convert_fusion
  19.0 0.0 copy-done.5
  19.1 1.3 convolution_convert_fusion.1
  20.4 1.5 pad_maximum_fusion
  21.9 2.9 copy.38
  24.8 0.0 all-to-all-done
  24.8 0.1 copy.30
  24.9 0.1 reshape.58
  25.0 0.1 copy.28
  25.1 0.1 copy.29
  25.2 4.8 %gather_fusion = bf16[32,128,1024]{2,1,0:T(8,128)(2,1)} fusion(bf16[8,128,1024]{2,1,0:T(8,128)(2,1)S(1)} %bitcast.34, s32[1024]{0:T(1024)S(1)} %pad_clamp_fusion), kind=kCustom, calls=%fused_computation | custom fusion | bytes 16777344 | tf_op jit(solution)/shard_map/jit(_take)/gather | solution.py:53
  30.0 7.5 %copy_select_fusion = bf16[2,16,128,1024]{3,2,0,1:T(8,128)(2,1)} fusion(bf16[2,16,128,1024]{3,2,1,0:T(8,128)(2,1)} %bitcast.35, pred[2,16]{0,1:T(8,128)(4,1)S(1)} %copy.29), kind=kLoop, calls=%fused_computation.2 | loop fusion | flops 4194304 | bytes 16777248 | tf_op jit(solution)/shard_map/jit(_take)/select_n | solution.py:53
  37.5 0.0 copy-start.6
  37.5 0.0 copy-start.2
  37.5 0.0 copy-start.4
  37.5 7.1 %all-to-all-start.1 = ((bf16[2,16,128,1024]{3,2,0,1:T(8,128)(2,1)}), bf16[2,16,128,1024]{3,2,0,1:T(8,128)(2,1)}, u32[]{:S(2)}, u32[]{:S(2)}) async-start(bf16[2,16,128,1024]{3,2,0,1:T(8,128)(2,1)} %copy_select_fusion), calls=%async_computation.1 | async-start | bytes 16777216 | tf_op jit(solution)/shard_map/all_to_all | solution.py:54
  44.6 0.2 reduce-scatter.2.cloned.1.call-start
  44.8 0.0 copy-done.6
  44.8 0.1 iota_compare_fusion.1
  44.9 0.1 fusion.24
  45.0 0.1 broadcast_bitcast_fusion
  45.1 0.0 copy-done.2
  45.1 0.0 copy-done.4
  45.1 0.4 convolution_convert_fusion.2
  45.5 0.1 reshape.53
  45.6 154.6 %all-to-all-done.1 = bf16[2,16,128,1024]{3,2,0,1:T(8,128)(2,1)} async-done(((bf16[2,16,128,1024]{3,2,0,1:T(8,128)(2,1)}), bf16[2,16,128,1024]{3,2,0,1:T(8,128)(2,1)}, u32[]{:S(2)}, u32[]{:S(2)}) %all-to-all-start.1) | async-done | bytes 8388640 | tf_op jit(solution)/shard_map/all_to_all | solution.py:54
  200.2 12.6 %copy.33 = bf16[2,16,128,1024]{2,1,3,0:T(8,128)(2,1)} copy(bf16[2,16,128,1024]{3,2,0,1:T(8,128)(2,1)} %all-to-all-done.1) | data formatting | bytes 16777216 | tf_op jit(solution)/shard_map/all_to_all | solution.py:54
  212.8 13.3 %reshape.51 = bf16[2,2048,1024]{1,2,0:T(8,128)(2,1)} reshape(bf16[2,16,128,1024]{2,1,3,0:T(8,128)(2,1)} %copy.33) | data formatting | bytes 16777216 | tf_op jit(solution)/shard_map/reshape | solution.py:57
  226.1 6.0 %fusion.27 = (bf16[2,2048,512]{1,2,0:T(8,128)(2,1)}, bf16[2,2048,512]{1,2,0:T(8,128)(2,1)}) fusion(bf16[2,2048,1024]{1,2,0:T(8,128)(2,1)} %reshape.51), kind=kLoop, calls=%fused_computation.44 | loop fusion | bytes 16777216 | tf_op jit(solution)/shard_map/slice | solution.py:13
  232.1 10.6 %fusion.28 = (f32[2,4,128]{2,1,0:T(4,128)S(1)}, f32[2,4,128,2048]{3,2,1,0:T(8,128)}) fusion(pred[2,2048]{1,0:T(4,128)(4,1)S(1)} %bitcast.39, bf16[2,2048,4,128]{1,3,2,0:T(8,128)(2,1)} %bitcast.37, bf16[2,128,4,128]{3,2,1,0:T(4,128)(2,1)S(1)} %reshape.53), kind=kOutput, calls=%fused_computation.45 | convolution fusion | flops 1086326784 | bytes 12853248 | tf_op jit(solution)/shard_map/sub | solution.py:21
  242.7 0.0 copy-start.3
  242.7 0.0 copy-start.1
  242.7 6.8 %fusion.10 = bf16[2,128,4,128]{1,3,2,0:T(8,128)(2,1)} fusion(bf16[2,2048,4,128]{1,3,2,0:T(8,128)(2,1)} %bitcast.36, f32[2,4,128,2048]{3,2,1,0:T(8,128)} %get-tuple-element.12, f32[2,4,128]{2,1,0:T(4,128)S(1)} %get-tuple-element.11), kind=kOutput, calls=%fused_computation.17 | convolution fusion | flops 541196288 | bytes 12849152 | tf_op jit(solution)/shard_map/qhik,qkhd->qihd/dot_general | solution.py:23
  249.5 1.1 copy.36
  250.6 0.0 copy-done.3
  250.7 1.4 fusion.13
  252.1 0.0 reduce-scatter.2.cloned.1.call-update
  252.1 42.3 %reduce-scatter.2.cloned.1.call-done = f32[256,512]{1,0:T(8,128)} async-done(((f32[256,1024]{1,0:T(8,128)}), f32[256,512]{1,0:T(8,128)}) %reduce-scatter.2.cloned.1.call-update) | async-done | bytes 524304 | tf_op jit(solution)/shard_map/reduce_scatter | solution.py:62
  294.4 1.8 convert_element_type.27
  296.2 0.0 copy-done.1
  (3 shorter events, 0.0 us)
Async XLA Ops:
  6.5 10.0 %copy-start = (bf16[1024,1024]{1,0:T(8,128)(2,1)S(1)}, bf16[1024,1024]{1,0:T(8,128)(2,1)}, u32[]{:S(2)}) copy-start(bf16[1024,1024]{1,0:T(8,128)(2,1)} %param.9) | copy-start | bytes 6291460
  6.5 12.5 %copy-start.5 = (bf16[1024,512]{1,0:T(8,128)(2,1)S(1)}, bf16[1024,512]{1,0:T(8,128)(2,1)}, u32[]{:S(2)}) copy-start(bf16[1024,512]{1,0:T(8,128)(2,1)} %param.11) | copy-start | bytes 3145732
  8.2 16.6 %all-to-all-start = ((s32[2,16,1]{0,2,1:T(1,128)}), s32[2,16,1]{0,2,1:T(1,128)S(1)}, u32[]{:S(2)}, u32[]{:S(2)}) async-start(s32[2,16,1]{0,2,1:T(1,128)} %copy.27), calls=%async_computation | async-start | bytes 16384 | tf_op jit(solution)/shard_map/all_to_all | solution.py:52
  37.5 7.3 %copy-start.6 = (s32[2]{0:T(128)S(1)}, s32[2]{0:T(128)}, u32[]{:S(2)}) copy-start(s32[2]{0:T(128)} %param.15) | copy-start | bytes 28
  37.5 7.6 %copy-start.2 = (bf16[1024,512]{1,0:T(8,128)(2,1)S(1)}, bf16[1024,512]{1,0:T(8,128)(2,1)}, u32[]{:S(2)}) copy-start(bf16[1024,512]{1,0:T(8,128)(2,1)} %param.10) | copy-start | bytes 3145732
  37.5 7.6 %copy-start.4 = (bf16[256,1024]{1,0:T(8,128)(2,1)S(1)}, bf16[256,1024]{1,0:T(8,128)(2,1)}, u32[]{:S(2)}) copy-start(bf16[256,1024]{1,0:T(8,128)(2,1)} %param.8) | copy-start | bytes 1572868
  37.5 162.7 %all-to-all-start.1 = ((bf16[2,16,128,1024]{3,2,0,1:T(8,128)(2,1)}), bf16[2,16,128,1024]{3,2,0,1:T(8,128)(2,1)}, u32[]{:S(2)}, u32[]{:S(2)}) async-start(bf16[2,16,128,1024]{3,2,0,1:T(8,128)(2,1)} %copy_select_fusion), calls=%async_computation.1 | async-start | bytes 16777216 | tf_op jit(solution)/shard_map/all_to_all | solution.py:54
  44.6 249.9 %reduce-scatter.2.cloned.1.call-start = ((), (), s32[]{:S(2)}) async-start(), calls=%async_computation.3 | async-start | bytes 1572864 | tf_op jit(solution)/shard_map/reduce_scatter | solution.py:62
  242.7 8.0 %copy-start.3 = (bf16[512,1024]{1,0:T(8,128)(2,1)S(1)}, bf16[512,1024]{1,0:T(8,128)(2,1)}, u32[]{:S(2)}) copy-start(bf16[512,1024]{1,0:T(8,128)(2,1)} %param.13) | copy-start | bytes 3145732
  242.7 53.6 %copy-start.1 = (bf16[1024,1024]{1,0:T(8,128)(2,1)S(1)}, bf16[1024,1024]{1,0:T(8,128)(2,1)}, u32[]{:S(2)}) copy-start(bf16[1024,1024]{1,0:T(8,128)(2,1)} %param.9) | copy-start | bytes 6291460
Sparse Core Ops, SparseCore 0:
  252.2 42.1 reduce-scatter.1
where the time goes:
time: 304 us; the launch traced here: 303 us
  waiting for transfers between devices  197 us (65%)
  local copies, waits for them, and re-layouts  41.9 us (14%)
  matrix products  23.1 us (8%)
  starting transfers between devices  15.6 us (5%)
  between operations  13.5 us (4%)
  other arithmetic  11.9 us (4%)
    all_to_all x1, waiting for transfers between devices, per_device(): lax.all_to_all(picked, 'view', split_axis=1, concat_axis=1, tiled=True)  155 us
    reduce_scatter x1, waiting for transfers between devices, per_device(): lax.psum_scatter(partial_value, 'head', scatter_dimension=1, tiled=True)  42.3 us
    reshape x1, local copies, waits for them, and re-layouts, per_device(): key_rows = arrived.reshape(groups, -1, 2 * panel_width)  13.3 us
    all_to_all x1, local copies, waits for them, and re-layouts, per_device(): lax.all_to_all(picked, 'view', split_axis=1, concat_axis=1, tiled=True)  12.6 us
    sub x1, matrix products, attend(): raised = jnp.where(allowed, jnp.exp(scores - peak), 0.0)  10.6 us
    all_to_all x1, starting transfers between devices, per_device(): lax.all_to_all(wanted, 'view', split_axis=1, concat_axis=1, tiled=True)  8.34 us
    select_n x1, other arithmetic, per_device(): picked = jnp.take(image_tiles, asked_ids, axis=0)  7.47 us
    all_to_all x1, starting transfers between devices, per_device(): lax.all_to_all(picked, 'view', split_axis=1, concat_axis=1, tiled=True)  7.08 us
  transfers between devices with their start and end apart: 3, of which 2 were waited for; matrix products, arithmetic and copies ran while one was open for 3% of the time, Pallas kernels for 0%

commit v1 on v0

--- a/solution.py
+++ b/solution.py
@@ -6,6 +6,13 @@
 
 HEAD_DIM = 128
 BLOCK = 128
+
+
+def swap_blocks(x, axis, split, join):
+    size = lax.axis_size(axis)
+    tiles = jnp.stack(jnp.split(x, size, axis=split), axis=0)
+    tiles = lax.all_to_all(tiles, axis, split_axis=0, concat_axis=0)
+    return jnp.concatenate(tiles, axis=join)
 
 
 def attend(query_heads, key_rows, visible, panel_width, head_count):
@@ -51,7 +58,7 @@
     sourced = jnp.any(matches & listed[:, :, None], axis=1)
     asked_ids = lax.all_to_all(wanted, "view", split_axis=1, concat_axis=1, tiled=True)
     picked = jnp.take(image_tiles, asked_ids, axis=0)
-    arrived = lax.all_to_all(picked, "view", split_axis=1, concat_axis=1, tiled=True)
+    arrived = swap_blocks(picked, "view", 1, 1)
     groups = arrived.shape[0]
     query_heads = queries.reshape(query_blocks, BLOCK, head_count, HEAD_DIM)
     key_rows = arrived.reshape(groups, -1, 2 * panel_width)

time: 304 us -> 330 us (1.086)
  local copies, waits for them, and re-layouts: 41.9 us -> 66.6 us
    unnamed x16 -> x29, local copies, waits for them, and re-layouts: 0.12 us -> 28.2 us
    all_to_all x1 -> x0, local copies, waits for them, and re-layouts: 12.6 us -> none  [per_device(): lax.all_to_all(picked, 'view', split_axis=1, concat_axis=1, tiled=True)]
    slice x0 -> x1, local copies, waits for them, and re-layouts: none -> 6.31 us  [attend(): key_rows[:, :, panel_width:].reshape(groups, length, head_count, HEAD_DIM)]
    slice x1 -> x2, local copies, waits for them, and re-layouts: 6 us -> 12 us  [attend(): key_rows[:, :, :panel_width].reshape(groups, length, head_count, HEAD_DIM)]
    reshape x1, local copies, waits for them, and re-layouts: 13.3 us -> 8.25 us  [swap_blocks(): return jnp.concatenate(tiles, axis=join)]
where the time goes in v1:
time: 330 us; the launch traced here: 329 us
  waiting for transfers between devices  197 us (60%)
  local copies, waits for them, and re-layouts  66.6 us (20%)
  matrix products  24.2 us (7%)
  starting transfers between devices  15.7 us (5%)
  between operations  13.5 us (4%)
  other arithmetic  11.9 us (4%)
    all_to_all x1, waiting for transfers between devices, swap_blocks(): tiles = lax.all_to_all(tiles, axis, split_axis=0, concat_axis=0)  155 us
    reduce_scatter x1, waiting for transfers between devices, per_device(): lax.psum_scatter(partial_value, 'head', scatter_dimension=1, tiled=True)  42.4 us
    unnamed x29, local copies, waits for them, and re-layouts  28.2 us
    slice x2, local copies, waits for them, and re-layouts, attend(): key_rows[:, :, :panel_width].reshape(groups, length, head_count, HEAD_DIM)  12 us
    sub x1, matrix products, attend(): raised = jnp.where(allowed, jnp.exp(scores - peak), 0.0)  10.5 us
    all_to_all x1, starting transfers between devices, per_device(): lax.all_to_all(wanted, 'view', split_axis=1, concat_axis=1, tiled=True)  8.34 us
    reshape x1, local copies, waits for them, and re-layouts, swap_blocks(): return jnp.concatenate(tiles, axis=join)  8.25 us
    select_n x1, other arithmetic, per_device(): picked = jnp.take(image_tiles, asked_ids, axis=0)  7.47 us
  transfers between devices with their start and end apart: 3, of which 2 were waited for; matrix products, arithmetic and copies ran while one was open for 3% of the time, Pallas kernels for 0%

profile of v1, /device:TPU:0, one launch (start us, length us, event | category | flops | bytes accessed | tf_op | source)
XLA Modules:
  0.0 328.9 jit_solution(3050426945798820937)
XLA Ops:
  6.5 0.0 copy-start
  6.5 0.8 and_select_fusion.1
  7.4 0.1 select_reduce_fusion.1
  7.5 0.7 copy.54
  8.2 8.3 %all-to-all-start = ((s32[2,16,1]{0,2,1:T(1,128)}), s32[2,16,1]{0,2,1:T(1,128)S(1)}, u32[]{:S(2)}, u32[]{:S(2)}) async-start(s32[2,16,1]{0,2,1:T(1,128)} %copy.54), calls=%async_computation | async-start | bytes 16384 | tf_op jit(solution)/shard_map/all_to_all | solution.py:59
  16.5 0.0 copy-done
  16.5 2.5 convolution_convert_fusion
  19.0 2.5 convolution_convert_fusion.1
  21.6 1.5 pad_maximum_fusion
  23.1 2.9 copy.67
  25.9 0.0 all-to-all-done
  26.0 0.1 copy.57
  26.0 0.1 reshape.58
  26.1 0.1 copy.55
  26.2 0.1 copy.56
  26.3 4.8 %gather_fusion = bf16[32,128,1024]{2,1,0:T(8,128)(2,1)} fusion(bf16[8,128,1024]{2,1,0:T(8,128)(2,1)S(1)} %bitcast.96, s32[1024]{0:T(1024)S(1)} %pad_clamp_fusion), kind=kCustom, calls=%fused_computation | custom fusion | bytes 16777344 | tf_op jit(solution)/shard_map/jit(_take)/gather | solution.py:60
  31.2 7.5 %copy_select_fusion = bf16[2,16,128,1024]{3,2,0,1:T(8,128)(2,1)} fusion(bf16[2,16,128,1024]{3,2,1,0:T(8,128)(2,1)} %bitcast.97, pred[2,16]{0,1:T(8,128)(4,1)S(1)} %copy.56), kind=kLoop, calls=%fused_computation.2 | loop fusion | flops 4194304 | bytes 16777248 | tf_op jit(solution)/shard_map/jit(_take)/select_n | solution.py:60
  38.6 1.9 fusion.28
  40.5 1.9 fusion.27
  42.4 1.9 fusion.26
  44.3 1.9 fusion.25
  46.1 1.9 fusion.24
  48.0 1.9 fusion.23
  49.9 1.9 fusion.22
  51.7 1.9 fusion.21
  53.6 1.9 fusion.20
  55.5 1.9 fusion.19
  57.4 1.9 fusion.18
  59.3 1.9 fusion.17
  61.1 1.9 fusion.16
  63.0 1.9 fusion.15
  64.9 1.9 fusion.14
  66.8 1.9 fusion.13
  68.7 0.0 copy-start.5
  68.7 0.0 copy-start.2
  68.7 0.0 copy-start.4
  68.7 7.1 %all-to-all-start.1 = ((bf16[16,2,1,128,1024]{4,3,1,2,0:T(8,128)(2,1)}), bf16[16,2,1,128,1024]{4,3,1,2,0:T(8,128)(2,1)}, u32[]{:S(2)}, u32[]{:S(2)}) async-start(bf16[16,2,1,128,1024]{4,3,1,2,0:T(8,128)(2,1)} %fusion.13), calls=%async_computation.1 | async-start | bytes 16777216 | tf_op jit(solution)/shard_map/all_to_all | solution.py:14
  75.8 0.2 reduce-scatter.2.cloned.1.call-start
  76.0 0.0 copy-done.5
  76.0 0.1 iota_compare_fusion.1
  76.1 0.1 fusion.40
  76.2 0.1 broadcast_bitcast_fusion
  76.3 0.0 copy-done.2
  76.3 0.0 copy-done.4
  76.3 0.4 convolution_convert_fusion.2
  76.7 0.1 reshape.53
  76.8 154.5 %all-to-all-done.1 = bf16[16,2,1,128,1024]{4,3,1,2,0:T(8,128)(2,1)} async-done(((bf16[16,2,1,128,1024]{4,3,1,2,0:T(8,128)(2,1)}), bf16[16,2,1,128,1024]{4,3,1,2,0:T(8,128)(2,1)}, u32[]{:S(2)}, u32[]{:S(2)}) %all-to-all-start.1) | async-done | bytes 8388640 | tf_op jit(solution)/shard_map/all_to_all | solution.py:14
  231.3 8.3 %copy.60 = bf16[2,16,1,128,1024]{4,3,1,0,2:T(8,128)(2,1)} copy(bf16[2,16,1,128,1024]{4,3,0,2,1:T(8,128)(2,1)} %bitcast.20) | data formatting | bytes 16777216 | tf_op jit(solution)/shard_map/reshape | solution.py:15
  239.6 5.8 %fusion.43 = (bf16[2,2048,512]{2,1,0:T(8,128)(2,1)}, bf16[2,2048,512]{2,1,0:T(8,128)(2,1)}) fusion(bf16[2,2048,1024]{2,1,0:T(8,128)(2,1)} %bitcast.98), kind=kLoop, calls=%fused_computation.76 | loop fusion | bytes 16777216 | tf_op jit(solution)/shard_map/slice | solution.py:20
  245.3 6.2 %copy.62 = bf16[2,2048,512]{1,2,0:T(8,128)(2,1)} copy(bf16[2,2048,512]{2,1,0:T(8,128)(2,1)} %get-tuple-element.7) | data formatting | bytes 8388608 | tf_op jit(solution)/shard_map/slice | solution.py:20
  251.6 6.3 %copy.61 = bf16[2,2048,512]{1,2,0:T(8,128)(2,1)} copy(bf16[2,2048,512]{2,1,0:T(8,128)(2,1)} %get-tuple-element.8) | data formatting | bytes 8388608 | tf_op jit(solution)/shard_map/slice | solution.py:21
  257.9 10.5 %fusion.44 = (f32[2,4,128]{2,1,0:T(4,128)S(1)}, f32[2,4,128,2048]{3,2,1,0:T(8,128)}) fusion(pred[2,2048]{1,0:T(4,128)(4,1)S(1)} %bitcast.102, bf16[2,2048,4,128]{1,3,2,0:T(8,128)(2,1)} %bitcast.99, bf16[2,128,4,128]{3,2,1,0:T(4,128)(2,1)S(1)} %reshape.53), kind=kOutput, calls=%fused_computation.77 | convolution fusion | flops 1086326784 | bytes 12853248 | tf_op jit(solution)/shard_map/sub | solution.py:28
  268.4 0.0 copy-start.3
  268.4 0.0 copy-start.1
  268.4 6.8 %fusion.10 = bf16[2,128,4,128]{1,3,2,0:T(8,128)(2,1)} fusion(bf16[2,2048,4,128]{1,3,2,0:T(8,128)(2,1)} %bitcast.100, f32[2,4,128,2048]{3,2,1,0:T(8,128)} %get-tuple-element.12, f32[2,4,128]{2,1,0:T(4,128)S(1)} %get-tuple-element.11), kind=kOutput, calls=%fused_computation.17 | convolution fusion | flops 541196288 | bytes 12849152 | tf_op jit(solution)/shard_map/qhik,qkhd->qihd/dot_general | solution.py:30
  275.3 1.1 copy.65
  276.4 0.0 copy-done.3
  276.4 1.4 fusion.29
  277.8 0.0 reduce-scatter.2.cloned.1.call-update
  277.9 42.4 %reduce-scatter.2.cloned.1.call-done = f32[256,512]{1,0:T(8,128)} async-done(((f32[256,1024]{1,0:T(8,128)}), f32[256,512]{1,0:T(8,128)}) %reduce-scatter.2.cloned.1.call-update) | async-done | bytes 524304 | tf_op jit(solution)/shard_map/reduce_scatter | solution.py:69
  320.2 1.8 convert_element_type.27
  322.0 0.0 copy-done.1
  (3 shorter events, 0.0 us)
Async XLA Ops:
  6.5 10.0 %copy-start = (bf16[1024,1024]{1,0:T(8,128)(2,1)S(1)}, bf16[1024,1024]{1,0:T(8,128)(2,1)}, u32[]{:S(2)}) copy-start(bf16[1024,1024]{1,0:T(8,128)(2,1)} %param.9) | copy-start | bytes 6291460
  8.2 17.8 %all-to-all-start = ((s32[2,16,1]{0,2,1:T(1,128)}), s32[2,16,1]{0,2,1:T(1,128)S(1)}, u32[]{:S(2)}, u32[]{:S(2)}) async-start(s32[2,16,1]{0,2,1:T(1,128)} %copy.54), calls=%async_computation | async-start | bytes 16384 | tf_op jit(solution)/shard_map/all_to_all | solution.py:59
  68.7 7.3 %copy-start.5 = (s32[2]{0:T(128)S(1)}, s32[2]{0:T(128)}, u32[]{:S(2)}) copy-start(s32[2]{0:T(128)} %param.15) | copy-start | bytes 28
  68.7 7.6 %copy-start.2 = (bf16[1024,512]{1,0:T(8,128)(2,1)S(1)}, bf16[1024,512]{1,0:T(8,128)(2,1)}, u32[]{:S(2)}) copy-start(bf16[1024,512]{1,0:T(8,128)(2,1)} %param.10) | copy-start | bytes 3145732
  68.7 7.6 %copy-start.4 = (bf16[256,1024]{1,0:T(8,128)(2,1)S(1)}, bf16[256,1024]{1,0:T(8,128)(2,1)}, u32[]{:S(2)}) copy-start(bf16[256,1024]{1,0:T(8,128)(2,1)} %param.8) | copy-start | bytes 1572868
  68.7 162.7 %all-to-all-start.1 = ((bf16[16,2,1,128,1024]{4,3,1,2,0:T(8,128)(2,1)}), bf16[16,2,1,128,1024]{4,3,1,2,0:T(8,128)(2,1)}, u32[]{:S(2)}, u32[]{:S(2)}) async-start(bf16[16,2,1,128,1024]{4,3,1,2,0:T(8,128)(2,1)} %fusion.13), calls=%async_computation.1 | async-start | bytes 16777216 | tf_op jit(solution)/shard_map/all_to_all | solution.py:14
  75.8 244.5 %reduce-scatter.2.cloned.1.call-start = ((), (), s32[]{:S(2)}) async-start(), calls=%async_computation.3 | async-start | bytes 1572864 | tf_op jit(solution)/shard_map/reduce_scatter | solution.py:69
  268.4 8.0 %copy-start.3 = (bf16[512,1024]{1,0:T(8,128)(2,1)S(1)}, bf16[512,1024]{1,0:T(8,128)(2,1)}, u32[]{:S(2)}) copy-start(bf16[512,1024]{1,0:T(8,128)(2,1)} %param.13) | copy-start | bytes 3145732
  268.4 53.6 %copy-start.1 = (bf16[1024,1024]{1,0:T(8,128)(2,1)S(1)}, bf16[1024,1024]{1,0:T(8,128)(2,1)}, u32[]{:S(2)}) copy-start(bf16[1024,1024]{1,0:T(8,128)(2,1)} %param.9) | copy-start | bytes 6291460
Sparse Core Ops, SparseCore 0:
  278.0 42.2 reduce-scatter.1
